TPU v7x, 32 devices: a whole 2x2x4 slice. The times are simulated.
32 devices in a mesh: dp: 8 (over z, x), section: 4 (over y, core).
Axes of the slice: x: 2, y: 2, z: 4, core: 2. Of those that a mesh axis runs over, the one named last changes fastest.
Arguments:
- saved_inputs: bfloat16 [4, 6144, 1024], P('section', 'dp'), may hold values from -6 to 6
- cotangent: bfloat16 [6144, 1024], P('dp'), may hold values from -6 to 6
- pack_lists: int32 [8, 768], P('dp'), may hold values from 0 to 767, each once within a row
- segment_ids: int32 [96, 64], P('dp'), may hold values from 0 to 7, never falling along the last dimension, each value on 1 to 32 neighbouring positions
- w_in: bfloat16 [4, 1024, 4096], P('section'), may hold values from -0.1875 to 0.1875
- w_out: bfloat16 [4, 1024, 1024], P('section'), may hold values from -0.1875 to 0.1875
Outputs:
- grad_inputs: bfloat16 [4, 6144, 1024], P('section', 'dp')
- grad_w_in: float32 [4, 1024, 4096], P('section', 'dp')
- grad_w_out: float32 [4, 1024, 1024], P('section', 'dp')
Inputs may be any that keep to these rules, and one draw needn't show every extreme that they name: `pack_lists`: each row is an ordering of the rows of one loader rank; its k-th block of equal length names the rows sent to packed rank k. `segment_ids`: ids never fall along a micro-batch; a history is the run of one id, 1 to 32 rows, and one has exactly 32.
All inputs are finite; a program needn't handle non-finite values.
Results may differ from a plain program's by a relative error of at most 0.03.
Values may be sent and summed in bfloat16 or wider, within the bound.
A program may use at most 128 MiB of HBM per device.

v0:
```python
import functools

import jax
import jax.numpy as jnp
from jax import lax
from jax.experimental import pallas as pl
from jax.experimental.pallas import tpu as pltpu
from jax.sharding import PartitionSpec as P

H = 16
F_BATCHES = 3
B_BATCHES = 3
X_LAG = 2
Z_LAG = 4
BF = jnp.bfloat16
F32 = jnp.float32
VMEM_LIMIT = 60 * 1024 * 1024


def mm(a, b):
    return lax.dot_general(a, b, (((1,), (0,)), ((), ())), preferred_element_type=F32)


def mm_t(a, b):
    return lax.dot_general(a, b, (((1,), (1,)), ((), ())), preferred_element_type=F32)


def t_mm(a, b):
    return lax.dot_general(a, b, (((0,), (0,)), ((), ())), preferred_element_type=F32)


def sigmoid(x):
    return 0.5 * jnp.tanh(0.5 * x) + 0.5


def stacked(part, mask, copies):
    return jnp.concatenate([part] * copies, axis=0) * mask


def norm_stats(values):
    centered = values - jnp.mean(values, axis=-1, keepdims=True)
    variance = jnp.mean(centered * centered, axis=-1, keepdims=True)
    inv = lax.rsqrt(variance + 1e-05)
    return centered * inv, inv


def forward_kernel(
    rows, dp_count, sections, x_ref, w_ref, mask_ref, bm_ref, picked_ref,
    win_part_ref, wout_part_ref,
    packed_ref, xy_ref, gate_ref, mhat_ref, vqk_ref, slope_ref, att_ref, sfac_ref, rx_ref, rm_ref,
    win_t_ref, wout_t_ref, send_sem, recv_sem, own_sem,
):
    step = pl.program_id(0)
    sender = lax.axis_index("section") == sections - 1
    me = lax.axis_index("dp")
    own = pltpu.make_async_copy(picked_ref.at[me], packed_ref.at[me], own_sem)

    def hop(offset):
        peer = (me + offset) % dp_count
        return pltpu.make_async_remote_copy(
            src_ref=picked_ref.at[peer],
            dst_ref=packed_ref.at[me],
            send_sem=send_sem.at[offset - 1],
            recv_sem=recv_sem.at[offset - 1],
            device_id={"dp": peer},
            device_id_type=pl.DeviceIdType.MESH,
        )

    @pl.when((step == 0) & sender)
    def _():
        barrier = pltpu.get_barrier_semaphore()
        for offset in range(1, dp_count):
            pl.semaphore_signal(
                barrier, inc=1, device_id={"dp": (me + offset) % dp_count},
                device_id_type=pl.DeviceIdType.MESH,
            )
        pl.semaphore_wait(barrier, dp_count - 1)
        own.start()
        for offset in range(1, dp_count):
            hop(offset).start()

    width = x_ref.shape[1]
    group = bm_ref.shape[0]
    copies = group // rows
    head_dim = width // H
    xn, rx = norm_stats(x_ref[...].astype(F32))
    xy_ref[:, :width] = xn.astype(BF)
    rx_ref[...] = jnp.broadcast_to(rx, rx_ref.shape)
    win_t_ref[...] = win_part_ref[...].T
    wout_t_ref[...] = wout_part_ref[...].T
    for part in range(4):
        cols = slice(part * width, (part + 1) * width)
        pre = mm(xy_ref[:, :width], w_ref[:, cols])
        sig = sigmoid(pre)
        act = pre * sig
        slope_ref[:, cols] = (sig + act * (1.0 - sig)).astype(BF)
        if part == 0:
            gate_ref[...] = act.astype(BF)
        else:
            vqk_ref[:, (part - 1) * width : part * width] = act.astype(BF)
    block_mask = bm_ref[...]
    scale = 1.0 / head_dim ** 0.5
    for micro in range(x_ref.shape[0] // rows):
        r = slice(micro * rows, (micro + 1) * rows)
        allowed = jnp.concatenate([mask_ref[r, :]] * (group // mask_ref.shape[1]), axis=1)
        mixed = []
        for lo in range(0, width, group):
            c = slice(lo, lo + group)
            v = vqk_ref[r, lo : lo + group]
            q = vqk_ref[r, width + lo : width + lo + group]
            k = vqk_ref[r, 2 * width + lo : 2 * width + lo + group]
            scores = mm_t(q, stacked(k, block_mask, copies)) * scale
            sig = sigmoid(scores)
            act = scores * sig
            att = (act * allowed).astype(BF)
            att_ref[r, c] = att
            sfac_ref[r, c] = ((sig + act * (1.0 - sig)) * allowed * scale).astype(BF)
            mixed.append(mm(att, stacked(v, block_mask, copies)))
        mixed = jnp.concatenate(mixed, axis=1)
        mhat, rm = norm_stats(mixed)
        mhat_ref[r, :] = mhat.astype(BF)
        rm_ref[r, :] = jnp.broadcast_to(rm, (rows, rm_ref.shape[1]))
        xy_ref[r, width:] = (mhat * gate_ref[r, :].astype(F32)).astype(BF)

    @pl.when((step == pl.num_programs(0) - 1) & sender)
    def _():
        own.wait()
        for offset in range(1, dp_count):
            back = pltpu.make_async_remote_copy(
                src_ref=picked_ref.at[me],
                dst_ref=packed_ref.at[(me + dp_count - offset) % dp_count],
                send_sem=send_sem.at[offset - 1],
                recv_sem=recv_sem.at[offset - 1],
                device_id={"dp": (me + offset) % dp_count},
                device_id_type=pl.DeviceIdType.MESH,
            )
            back.wait_recv()
            hop(offset).wait_send()


def backward_kernel(
    rows, sections, g0_ref, win_ref, wout_ref, bm_ref, xn_ref, gate_ref, mhat_ref, vqk_ref,
    slope_ref, att_ref, sfac_ref, rx_ref, rm_ref,
    dx_ref, dpre_ref, arrived, leaving, send_sem, recv_sem,
):
    step = pl.program_id(0)
    steps = pl.num_programs(0)
    section = lax.axis_index("section")
    last = sections - 1
    width = g0_ref.shape[1]
    wide = 4 * width
    group = bm_ref.shape[0]
    copies = group // rows
    before = jnp.maximum(section - 1, 0)
    after = jnp.minimum(section + 1, last)

    def hop(slot):
        return pltpu.make_async_remote_copy(
            src_ref=leaving.at[slot],
            dst_ref=arrived.at[slot],
            send_sem=send_sem.at[slot],
            recv_sem=recv_sem.at[slot],
            device_id={"section": before},
            device_id_type=pl.DeviceIdType.MESH,
        )

    @pl.when(step == 0)
    def _():
        barrier = pltpu.get_barrier_semaphore()

        @pl.when(section > 0)
        def _():
            pl.semaphore_signal(
                barrier, inc=1, device_id={"section": before}, device_id_type=pl.DeviceIdType.MESH
            )

        @pl.when(section < last)
        def _():
            pl.semaphore_signal(
                barrier, inc=1, device_id={"section": after}, device_id_type=pl.DeviceIdType.MESH
            )

        peers = (section > 0).astype(jnp.int32) + (section < last).astype(jnp.int32)
        pl.semaphore_wait(barrier, peers)

    @pl.when(section == last)
    def _():
        dpre_ref[:, wide:] = g0_ref[...]

    @pl.when(section < last)
    def _():
        hop(step).wait_recv()
        dpre_ref[:, wide:] = arrived[step]

    gyu = mm(dpre_ref[:, wide:], wout_ref[...]).astype(BF).astype(F32)
    dpre_ref[:, :width] = (gyu * mhat_ref[...].astype(F32) * slope_ref[:, :width].astype(F32)).astype(BF)
    block_mask = bm_ref[...]
    block_mask_f = block_mask.astype(F32)

    def fold(full):
        full = full * block_mask_f
        total = full[:rows]
        for copy in range(1, copies):
            total = total + full[copy * rows : (copy + 1) * rows]
        return total.astype(BF).astype(F32)

    for micro in range(g0_ref.shape[0] // rows):
        r = slice(micro * rows, (micro + 1) * rows)
        dn = gyu[r, :] * gate_ref[r, :].astype(F32)
        mhat = mhat_ref[r, :].astype(F32)
        mean_d = jnp.mean(dn, axis=-1, keepdims=True)
        mean_p = jnp.mean(dn * mhat, axis=-1, keepdims=True)
        dm = (rm_ref[r, :1] * (dn - mean_d - mhat * mean_p)).astype(BF)
        for lo in range(0, width, group):
            c = slice(lo, lo + group)
            cv = slice(lo, lo + group)
            cq = slice(width + lo, width + lo + group)
            ck = slice(2 * width + lo, 2 * width + lo + group)
            dmg = dm[:, lo : lo + group]
            datt = mm_t(dmg, stacked(vqk_ref[r, cv], block_mask, copies)).astype(BF).astype(F32)
            ds = (datt * sfac_ref[r, c].astype(F32)).astype(BF)
            dv = fold(t_mm(att_ref[r, c], dmg))
            dq = mm(ds, stacked(vqk_ref[r, ck], block_mask, copies)).astype(BF).astype(F32)
            dk = fold(t_mm(ds, vqk_ref[r, cq]))
            for part, value in ((1, dv), (2, dq), (3, dk)):
                cols = slice(part * width + lo, part * width + lo + group)
                dpre_ref[r, cols] = (value * slope_ref[r, cols].astype(F32)).astype(BF)
    dn = mm(dpre_ref[:, :wide], win_ref[...])
    xn = xn_ref[...].astype(F32)
    mean_d = jnp.mean(dn, axis=-1, keepdims=True)
    mean_p = jnp.mean(dn * xn, axis=-1, keepdims=True)
    dx = (dpre_ref[:, wide:].astype(F32) + rx_ref[:, :1] * (dn - mean_d - xn * mean_p)).astype(BF)
    dx_ref[...] = dx

    @pl.when(section > 0)
    def _():
        leaving[step] = dx
        hop(step).start()

    @pl.when((section > 0) & (step == steps - 1))
    def _():
        def finish(slot, carry):
            hop(slot).wait_send()
            return carry

        lax.fori_loop(0, steps, finish, 0)


def weight_kernel(
    nx, nz, tiles, in_tiles, left_ref, right_ref, win_ref, wout_ref,
    product, from_x, part, from_z, xs_sem, xr_sem, zs_sem, zr_sem,
):
    step = pl.program_id(0)
    me = lax.axis_index("dp")
    my_z = me // nx
    my_x = me % nx
    rows = win_ref.shape[0]

    def device(z, x):
        return {"dp": z * nx + x}

    def x_hop(tile, offset):
        peer = (my_x + offset) % nx
        return pltpu.make_async_remote_copy(
            src_ref=product.at[tile, peer],
            dst_ref=from_x.at[tile, offset - 1],
            send_sem=xs_sem.at[tile, offset - 1],
            recv_sem=xr_sem.at[tile, offset - 1],
            device_id=device(my_z, peer),
            device_id_type=pl.DeviceIdType.MESH,
        )

    def z_hop(tile, offset):
        peer = (my_z + offset) % nz
        return pltpu.make_async_remote_copy(
            src_ref=part.at[tile, peer],
            dst_ref=from_z.at[tile, offset - 1],
            send_sem=zs_sem.at[tile, offset - 1],
            recv_sem=zr_sem.at[tile, offset - 1],
            device_id=device(peer, my_x),
            device_id_type=pl.DeviceIdType.MESH,
        )

    @pl.when(step == 0)
    def _():
        barrier = pltpu.get_barrier_semaphore()
        for offset in range(1, nx):
            pl.semaphore_signal(
                barrier, inc=1, device_id=device(my_z, (my_x + offset) % nx),
                device_id_type=pl.DeviceIdType.MESH,
            )
        for offset in range(1, nz):
            pl.semaphore_signal(
                barrier, inc=1, device_id=device((my_z + offset) % nz, my_x),
                device_id_type=pl.DeviceIdType.MESH,
            )
        pl.semaphore_wait(barrier, nx + nz - 2)

    @pl.when(step < tiles)
    def _():
        full = t_mm(left_ref[...], right_ref[...]).astype(BF)
        for x in range(nx):
            for z in range(nz):
                at = (z * nx + x) * rows
                product[step, x, z * rows : (z + 1) * rows, :] = full[at : at + rows]
        for offset in range(1, nx):
            x_hop(step, offset).start()

    @pl.when((step >= X_LAG) & (step < tiles + X_LAG))
    def _():
        tile = step - X_LAG
        total = product[tile, my_x].astype(F32)
        for offset in range(1, nx):
            x_hop(tile, offset).wait_recv()
            total = total + from_x[tile, offset - 1].astype(F32)
        total = total.astype(BF)
        for z in range(nz):
            part[tile, z] = total[z * rows : (z + 1) * rows]
        for offset in range(1, nz):
            z_hop(tile, offset).start()

    def finish(tile):
        total = part[tile, my_z].astype(F32)
        for offset in range(1, nz):
            z_hop(tile, offset).wait_recv()
            total = total + from_z[tile, offset - 1].astype(F32)
        for offset in range(1, nx):
            x_hop(tile, offset).wait_send()
        for offset in range(1, nz):
            z_hop(tile, offset).wait_send()
        return total

    @pl.when((step >= Z_LAG) & (step < Z_LAG + in_tiles))
    def _():
        win_ref[...] = finish(step - Z_LAG)

    @pl.when(step >= Z_LAG + in_tiles)
    def _():
        wout_ref[...] = finish(step - Z_LAG)


def weight_grads(left, right, dp_count):
    tok_rows = left.shape[0]
    width = left.shape[1] // 2
    wide = 4 * width
    cols = width // 4
    in_tiles, tiles = wide // cols, (wide + width) // cols
    out_tiles = tiles - in_tiles
    nx = 1 << ((dp_count.bit_length() - 1) // 2)
    nz = dp_count // nx
    rows = width // dp_count
    return pl.pallas_call(
        functools.partial(weight_kernel, nx, nz, tiles, in_tiles),
        grid=(tiles + Z_LAG,),
        in_specs=[
            pl.BlockSpec((tok_rows, width), lambda t: (0, jnp.minimum(t, tiles - 1) // in_tiles)),
            pl.BlockSpec((tok_rows, cols), lambda t: (0, jnp.minimum(t, tiles - 1))),
        ],
        out_specs=[
            pl.BlockSpec((rows, cols), lambda t: (0, jnp.clip(t - Z_LAG, 0, in_tiles - 1))),
            pl.BlockSpec((rows, cols), lambda t: (0, jnp.clip(t - Z_LAG - in_tiles, 0, out_tiles - 1))),
        ],
        out_shape=[
            jax.ShapeDtypeStruct((rows, wide), F32),
            jax.ShapeDtypeStruct((rows, width), F32),
        ],
        scratch_shapes=[
            pltpu.VMEM((tiles, nx, nz * rows, cols), BF),
            pltpu.VMEM((tiles, nx - 1, nz * rows, cols), BF),
            pltpu.VMEM((tiles, nz, rows, cols), BF),
            pltpu.VMEM((tiles, nz - 1, rows, cols), BF),
            pltpu.SemaphoreType.DMA((tiles, nx - 1)),
            pltpu.SemaphoreType.DMA((tiles, nx - 1)),
            pltpu.SemaphoreType.DMA((tiles, nz - 1)),
            pltpu.SemaphoreType.DMA((tiles, nz - 1)),
        ],
        compiler_params=pltpu.CompilerParams(
            vmem_limit_bytes=VMEM_LIMIT, collective_id=1, has_side_effects=True
        ),
        name="weights",
    )(left, right)


def pick(count, most):
    while count % most:
        most -= 1
    return most


def body(saved_inputs, cotangent, pack_lists, segment_ids, w_in, w_out):
    dp_count = lax.axis_size("dp")
    section_count = lax.axis_size("section")
    tok_rows, width = cotangent.shape
    micro_count, rows = segment_ids.shape
    share = tok_rows // dp_count
    group = rows * (256 // (width // H))
    wide = 4 * width
    picked = cotangent[pack_lists[0]]
    positions = jnp.arange(rows)
    allowed = (segment_ids[:, :, None] == jnp.concatenate([segment_ids] * 2, axis=1)[:, None, :]) & (
        jnp.concatenate([positions] * 2)[None, None, :] <= positions[None, :, None]
    )
    mask = (allowed.astype(F32) / rows).reshape(tok_rows, 2 * rows)
    blocks = jnp.arange(group) // rows
    block_mask = (blocks[:, None] == blocks[None, :]).astype(BF)

    def row_spec(tile, cols):
        return pl.BlockSpec((tile, cols), lambda i: (i, 0))

    def whole_spec(shape):
        return pl.BlockSpec(shape, lambda i: (0, 0), pipeline_mode=pl.Buffered(1))

    def whole_spec3(shape):
        return pl.BlockSpec(shape, lambda i: (0, 0, 0), pipeline_mode=pl.Buffered(1))

    tile = rows * pick(micro_count, F_BATCHES)
    f_steps = tok_rows // tile
    cols = [
        (2 * width, BF), (width, BF), (width, BF), (3 * width, BF),
        (wide, BF), (width, BF), (width, BF), (128, F32), (128, F32),
    ]
    packed, xy, gate, mhat, vqk, slope, att, sfac, rx, rm, win_t, wout_t = pl.pallas_call(
        functools.partial(forward_kernel, rows, dp_count, section_count),
        grid=(tok_rows // tile,),
        in_specs=[
            row_spec(tile, width), whole_spec((width, wide)),
            row_spec(tile, 2 * rows), whole_spec((group, group)),
            whole_spec3((dp_count, share, width)),
            pl.BlockSpec((width, wide // f_steps), lambda i: (0, i)),
            pl.BlockSpec((width // f_steps, width), lambda i: (i, 0)),
        ],
        out_specs=[pl.BlockSpec(memory_space=pl.ANY)]
        + [row_spec(tile, n) for n, _ in cols]
        + [pl.BlockSpec((wide // f_steps, width), lambda i: (i, 0)),
           pl.BlockSpec((width, width // f_steps), lambda i: (0, i))],
        out_shape=[jax.ShapeDtypeStruct((dp_count, share, width), BF)]
        + [jax.ShapeDtypeStruct((tok_rows, n), t) for n, t in cols]
        + [jax.ShapeDtypeStruct((wide, width), BF), jax.ShapeDtypeStruct((width, width), BF)],
        scratch_shapes=[
            pltpu.SemaphoreType.DMA((dp_count - 1,)),
            pltpu.SemaphoreType.DMA((dp_count - 1,)),
            pltpu.SemaphoreType.DMA,
        ],
        compiler_params=pltpu.CompilerParams(
            vmem_limit_bytes=VMEM_LIMIT, collective_id=2, has_side_effects=True
        ),
        cost_estimate=pl.CostEstimate(
            flops=2 * tok_rows * width * wide, bytes_accessed=40 << 20, transcendentals=tok_rows * wide
        ),
        name="forward",
    )(
        saved_inputs[0], w_in[0], mask, block_mask, picked.reshape(dp_count, share, width),
        w_in[0], w_out[0],
    )

    tile = rows * pick(micro_count, B_BATCHES)
    steps = tok_rows // tile
    dx, dgrad = pl.pallas_call(
        functools.partial(backward_kernel, rows, section_count),
        grid=(steps,),
        in_specs=[
            row_spec(tile, width), whole_spec((wide, width)), whole_spec((width, width)),
            whole_spec((group, group)), row_spec(tile, width), row_spec(tile, width),
            row_spec(tile, width), row_spec(tile, 3 * width), row_spec(tile, wide),
            row_spec(tile, width), row_spec(tile, width), row_spec(tile, 128), row_spec(tile, 128),
        ],
        out_specs=[row_spec(tile, width), row_spec(tile, wide + width)],
        out_shape=[
            jax.ShapeDtypeStruct((tok_rows, width), BF),
            jax.ShapeDtypeStruct((tok_rows, wide + width), BF),
        ],
        scratch_shapes=[
            pltpu.VMEM((steps, tile, width), BF),
            pltpu.VMEM((steps, tile, width), BF),
            pltpu.SemaphoreType.DMA((steps,)),
            pltpu.SemaphoreType.DMA((steps,)),
        ],
        compiler_params=pltpu.CompilerParams(
            vmem_limit_bytes=VMEM_LIMIT, collective_id=0, has_side_effects=True
        ),
        name="backward",
    )(packed.reshape(tok_rows, width), win_t, wout_t, block_mask, xy, gate, mhat, vqk, slope, att, sfac, rx, rm)

    grad_w_in, grad_w_out = weight_grads(xy, dgrad, dp_count)
    return (dx[None], grad_w_in[None], grad_w_out[None])


def solution(mesh):
    return jax.shard_map(
        body,
        mesh=mesh,
        in_specs=(
            P("section", "dp", None),
            P("dp", None),
            P("dp", None),
            P("dp", None),
            P("section", None, None),
            P("section", None, None),
        ),
        out_specs=(P("section", "dp", None), P("section", "dp", None), P("section", "dp", None)),
        check_vma=False,
    )
```

profile of v0, /device:TPU:0, one launch (start us, length us, event | category | flops | bytes accessed | tf_op | source)
XLA Modules:
  0.0 219.7 jit_solution(8617135363988285154)
XLA Ops:
  0.6 0.0 copy-start
  0.7 0.1 pad_add_fusion.1
  0.7 0.8 fusion.2
  1.6 0.8 eq.37
  2.3 0.8 pad_add_fusion
  3.2 0.8 compare_convert_fusion.bm_ref
  3.9 0.9 fusion.1.mask_ref
  4.9 0.0 copy-done
  4.9 3.5 %gather_fusion = bf16[768,1024]{1,0:T(8,128)(2,1)} fusion(bf16[768,1024]{1,0:T(8,128)(2,1)S(1)} %copy-done, s32[1024]{0:T(1024)S(1)} %pad_clamp_fusion), kind=kCustom, calls=%fused_computation | custom fusion | bytes 3148800 | tf_op jit(solution)/shard_map/gather | solution.py:398
  8.4 30.2 %forward.1 = (bf16[8,96,1024]{2,1,0:T(8,128)(2,1)}, bf16[768,2048]{1,0:T(8,128)(2,1)}, bf16[768,1024]{1,0:T(8,128)(2,1)}, bf16[768,1024]{1,0:T(8,128)(2,1)}, bf1...) custom-call(bf16[768,1024]{1,0:T(8,128)(2,1)} %bitcast.26, ...), custom_call_target="tpu_custom_call" | custom-call | flops 6442450944 | bytes 41943040 | tf_op jit(solution)/shard_map/forward/pallas_call | solution.py:422
  38.6 53.3 %backward.1 = (bf16[768,1024]{1,0:T(8,128)(2,1)}, bf16[768,5120]{1,0:T(8,128)(2,1)}) custom-call(bf16[768,1024]{1,0:T(8,128)(2,1)} %bitcast.19, bf16[4096,1024]{1,0:T(8,128)(2,1)} %get-tuple-element.20.win_ref, bf16[1024,1024]{1,0:T(8,128)(2,1)} %get-tuple-element.21.wout_ref, bf16[256,256]{1,0:T(8,128)(2,1)} %compare_convert_fusion.bm_ref, ...), custom_call_target="tpu_custom_call" | custom-call | tf_op jit(solution)/shard_map/backward/pallas_call | solution.py:458
  92.0 0.0 copy-start.2
  92.0 123.3 %weights.1 = (f32[128,4096]{1,0:T(8,128)}, f32[128,1024]{1,0:T(8,128)}) custom-call(bf16[768,2048]{1,0:T(8,128)(2,1)} %get-tuple-element.22.xn_ref.left_ref, bf16[768,5120]{1,0:T(8,128)(2,1)} %get-tuple-element.32.right_ref), custom_call_target="tpu_custom_call" | custom-call | tf_op jit(solution)/shard_map/weights/pallas_call | solution.py:352
  215.3 0.0 copy-done.2
  215.3 0.0 copy-start.1
  215.3 1.1 copy.12
  216.5 1.0 copy-done.1
  217.5 0.0 copy-start.3
  217.5 1.3 copy.13
  218.8 0.1 copy-done.3
  218.9 0.8 copy.14
  (4 shorter events, 0.0 us)
Async XLA Ops:
  0.6 4.2 %copy-start = (bf16[768,1024]{1,0:T(8,128)(2,1)S(1)}, bf16[768,1024]{1,0:T(8,128)(2,1)}, u32[]{:S(2)}) copy-start(bf16[768,1024]{1,0:T(8,128)(2,1)} %param.7) | copy-start | bytes 4718596
  92.0 123.4 %copy-start.2 = (bf16[768,1024]{1,0:T(8,128)(2,1)S(1)}, bf16[768,1024]{1,0:T(8,128)(2,1)}, u32[]{:S(2)}) copy-start(bf16[768,1024]{1,0:T(8,128)(2,1)} %get-tuple-element.31) | copy-start | bytes 4718596
  215.3 2.2 copy-start.1
  217.5 1.4 copy-start.3
where the time goes:
time: 220 us
  Pallas kernels  207 us (94%)
  local copies, waits for them, and re-layouts  8.67 us (4%)
  other arithmetic  3.42 us (2%)
    pallas_call x1, Pallas kernels, weight_grads(): pl.pallas_call(functools.partial(weight_kernel, nx, nz, tiles, in_tiles),...  123 us
    pallas_call x1, Pallas kernels, body(): pl.pallas_call(functools.partial(backward_kernel, rows, section_count), g...  53.3 us
    pallas_call x1, Pallas kernels, body(): pl.pallas_call(functools.partial(forward_kernel, rows, dp_count, section_...  30.2 us

commit v1 on v0

--- a/solution.py
+++ b/solution.py
@@ -9,9 +9,9 @@
 
 H = 16
 F_BATCHES = 3
-B_BATCHES = 3
-X_LAG = 2
-Z_LAG = 4
+B_BATCHES = 2
+LAG = 1
+HOP_LAG = 3
 BF = jnp.bfloat16
 F32 = jnp.float32
 VMEM_LIMIT = 60 * 1024 * 1024
@@ -246,97 +246,197 @@
         lax.fori_loop(0, steps, finish, 0)
 
 
+class Line:
+    def __init__(self, count, me, device, at, own, landed, send_sem, recv_sem):
+        self.count, self.me, self.device, self.at = count, me, device, at
+        self.own, self.landed = own, landed
+        self.send_sem, self.recv_sem = send_sem, recv_sem
+
+    def base(self, me):
+        return self.count - me if me > 0 else 0
+
+    def copy(self, src, slot, shard, peer):
+        return pltpu.make_async_remote_copy(
+            src_ref=src,
+            dst_ref=self.landed.at[self.at, slot],
+            send_sem=self.send_sem.at[self.at, shard],
+            recv_sem=self.recv_sem.at[self.at, slot],
+            device_id=self.device(peer),
+            device_id_type=pl.DeviceIdType.MESH,
+        )
+
+    def arrive(self, slot):
+        self.copy(self.landed.at[self.at, slot], slot, 0, 0).wait_recv()
+
+    def start(self):
+        last = self.count - 1
+
+        @pl.when(self.me == 0)
+        def _():
+            for shard in range(last, 0, -1):
+                self.copy(self.own(shard), shard - 1, shard, 1).start()
+
+        @pl.when(self.me == last)
+        def _():
+            for shard in range(last):
+                self.copy(self.own(shard), self.base(last - 1) + shard, shard, last - 1).start()
+
+    def pass_on(self, slot, shard, to_slot, peer):
+        self.arrive(slot)
+        ref = self.landed.at[self.at, slot]
+        ref[...] = (ref[...].astype(F32) + self.own(shard)[...].astype(F32)).astype(BF)
+        self.copy(ref, to_slot, shard, peer).start()
+
+    def stage(self, number):
+        up, down = number, self.count - 1 - number
+
+        @pl.when(self.me == up)
+        def _():
+            for shard in range(self.count - 1, up, -1):
+                self.pass_on(shard - up, shard, shard - up - 1, up + 1)
+            self.arrive(0)
+
+        @pl.when(self.me == down)
+        def _():
+            for shard in range(down):
+                self.pass_on(self.base(down) + shard, shard, self.base(down - 1) + shard, down - 1)
+            self.arrive(self.base(down) + down)
+
+    def finish(self, out):
+        inner = (self.me > 0) & (self.me < self.count - 1)
+        total = self.own(self.me)[...].astype(F32) + self.landed[self.at, 0].astype(F32)
+        if self.count == 2:
+            out(total)
+        else:
+            @pl.when(inner)
+            def _():
+                out(total + self.landed[self.at, self.count].astype(F32))
+
+            @pl.when(jnp.logical_not(inner))
+            def _():
+                out(total)
+
+    def sent(self):
+        for offset in range(1, self.count):
+            shard = (self.me + offset) % self.count
+            self.copy(self.own(shard), 0, shard, 0).wait_send()
+
+
 def weight_kernel(
-    nx, nz, tiles, in_tiles, left_ref, right_ref, win_ref, wout_ref,
-    product, from_x, part, from_z, xs_sem, xr_sem, zs_sem, zr_sem,
+    nx, nz, tiles, in_tiles, z_tiles, left_ref, right_ref, win_ref, wout_ref,
+    x_own, x_first, x_second, z_own, z_first, z_second,
+    xs1, xr1, xs2, xr2, zs1, zr1, zs2, zr2,
 ):
     step = pl.program_id(0)
     me = lax.axis_index("dp")
     my_z = me // nx
     my_x = me % nx
     rows = win_ref.shape[0]
+    period = tiles // z_tiles
+    last_lag = LAG + HOP_LAG * (nx + nz - 2)
 
     def device(z, x):
         return {"dp": z * nx + x}
 
-    def x_hop(tile, offset):
-        peer = (my_x + offset) % nx
-        return pltpu.make_async_remote_copy(
-            src_ref=product.at[tile, peer],
-            dst_ref=from_x.at[tile, offset - 1],
-            send_sem=xs_sem.at[tile, offset - 1],
-            recv_sem=xr_sem.at[tile, offset - 1],
-            device_id=device(my_z, peer),
-            device_id_type=pl.DeviceIdType.MESH,
-        )
-
-    def z_hop(tile, offset):
-        peer = (my_z + offset) % nz
-        return pltpu.make_async_remote_copy(
-            src_ref=part.at[tile, peer],
-            dst_ref=from_z.at[tile, offset - 1],
-            send_sem=zs_sem.at[tile, offset - 1],
-            recv_sem=zr_sem.at[tile, offset - 1],
-            device_id=device(peer, my_x),
-            device_id_type=pl.DeviceIdType.MESH,
-        )
+    def on_x(peer):
+        return device(my_z, peer)
+
+    def on_z(peer):
+        return device(peer, my_x)
+
+    def is_z(tile):
+        return (tile % period == 0) & (tile // period < z_tiles)
+
+    def lines(kind, tile):
+        if kind == "z":
+            at = tile // period
+            first = Line(nz, my_z, on_z, at, lambda j: z_own.at[at, j], z_first, zs1, zr1)
+            second = Line(
+                nx, my_x, on_x, at, lambda j: z_own.at[at, my_z, pl.ds(j * rows, rows)], z_second, zs2, zr2
+            )
+        else:
+            at = tile - jnp.minimum((tile + period - 1) // period, z_tiles)
+            first = Line(nx, my_x, on_x, at, lambda j: x_own.at[at, j], x_first, xs1, xr1)
+            second = Line(
+                nz, my_z, on_z, at, lambda j: x_own.at[at, my_x, pl.ds(j * rows, rows)], x_second, xs2, xr2
+            )
+        return first, second
 
     @pl.when(step == 0)
     def _():
         barrier = pltpu.get_barrier_semaphore()
-        for offset in range(1, nx):
-            pl.semaphore_signal(
-                barrier, inc=1, device_id=device(my_z, (my_x + offset) % nx),
-                device_id_type=pl.DeviceIdType.MESH,
-            )
-        for offset in range(1, nz):
-            pl.semaphore_signal(
-                barrier, inc=1, device_id=device((my_z + offset) % nz, my_x),
-                device_id_type=pl.DeviceIdType.MESH,
-            )
-        pl.semaphore_wait(barrier, nx + nz - 2)
+        greeted = 0
+        for mine, count, to in ((my_x, nx, on_x), (my_z, nz, on_z)):
+            for has, peer in ((mine > 0, mine - 1), (mine < count - 1, mine + 1)):
+                @pl.when(has)
+                def _(peer=peer, to=to):
+                    pl.semaphore_signal(
+                        barrier, inc=1, device_id=to(peer), device_id_type=pl.DeviceIdType.MESH
+                    )
+
+                greeted = greeted + has.astype(jnp.int32)
+        pl.semaphore_wait(barrier, greeted)
 
     @pl.when(step < tiles)
     def _():
         full = t_mm(left_ref[...], right_ref[...]).astype(BF)
-        for x in range(nx):
+
+        @pl.when(is_z(step))
+        def _():
+            first, _second = lines("z", step)
             for z in range(nz):
-                at = (z * nx + x) * rows
-                product[step, x, z * rows : (z + 1) * rows, :] = full[at : at + rows]
-        for offset in range(1, nx):
-            x_hop(step, offset).start()
-
-    @pl.when((step >= X_LAG) & (step < tiles + X_LAG))
-    def _():
-        tile = step - X_LAG
-        total = product[tile, my_x].astype(F32)
-        for offset in range(1, nx):
-            x_hop(tile, offset).wait_recv()
-            total = total + from_x[tile, offset - 1].astype(F32)
-        total = total.astype(BF)
-        for z in range(nz):
-            part[tile, z] = total[z * rows : (z + 1) * rows]
-        for offset in range(1, nz):
-            z_hop(tile, offset).start()
-
-    def finish(tile):
-        total = part[tile, my_z].astype(F32)
-        for offset in range(1, nz):
-            z_hop(tile, offset).wait_recv()
-            total = total + from_z[tile, offset - 1].astype(F32)
-        for offset in range(1, nx):
-            x_hop(tile, offset).wait_send()
-        for offset in range(1, nz):
-            z_hop(tile, offset).wait_send()
-        return total
-
-    @pl.when((step >= Z_LAG) & (step < Z_LAG + in_tiles))
-    def _():
-        win_ref[...] = finish(step - Z_LAG)
-
-    @pl.when(step >= Z_LAG + in_tiles)
-    def _():
-        wout_ref[...] = finish(step - Z_LAG)
+                z_own[first.at, z] = full[z * nx * rows : (z + 1) * nx * rows]
+            first.start()
+
+        @pl.when(jnp.logical_not(is_z(step)))
+        def _():
+            first, _second = lines("x", step)
+            for x in range(nx):
+                for z in range(nz):
+                    at = (z * nx + x) * rows
+                    x_own[first.at, x, z * rows : (z + 1) * rows, :] = full[at : at + rows]
+            first.start()
+
+    def work(kind, tile, lag):
+        n1 = nz if kind == "z" else nx
+        n2 = nx if kind == "z" else nz
+        first, second = lines(kind, tile)
+        number = (lag - LAG) // HOP_LAG
+        if 1 <= number <= n1 - 1:
+            first.stage(number)
+            if number == n1 - 1:
+                mine = first.own(first.me)
+
+                def keep(total):
+                    mine[...] = total.astype(BF)
+
+                first.finish(keep)
+                second.start()
+        elif number >= n1:
+            second.stage(number - n1 + 1)
+            if number == n1 + n2 - 2:
+                def put(total):
+                    @pl.when(tile < in_tiles)
+                    def _():
+                        win_ref[...] = total
+
+                    @pl.when(tile >= in_tiles)
+                    def _():
+                        wout_ref[...] = total
+
+                second.finish(put)
+                first.sent()
+                second.sent()
+
+    for lag in range(last_lag, LAG, -HOP_LAG):
+        tile = step - lag
+        live = (tile >= 0) & (tile < tiles)
+        for kind in ("z", "x"):
+            match = is_z(tile) if kind == "z" else jnp.logical_not(is_z(tile))
+
+            @pl.when(live & match)
+            def _(kind=kind, tile=tile, lag=lag):
+                work(kind, tile, lag)
 
 
 def weight_grads(left, right, dp_count):
@@ -349,31 +449,44 @@
     nx = 1 << ((dp_count.bit_length() - 1) // 2)
     nz = dp_count // nx
     rows = width // dp_count
+    px, pz = (nx - 1) / nx, (nz - 1) / nz
+    x_share = (pz - px / nz) / (px * (1 - 1 / nz) + pz * (1 - 1 / nx))
+    z_tiles = max(1, int(tiles * (1 - x_share) + 0.9))
+    x_tiles = tiles - z_tiles
+    last_lag = LAG + HOP_LAG * (nx + nz - 2)
+
+    def slots(count):
+        return count + 1 if count > 2 else 1
+
+    def buffers(count, n1, n2):
+        return [
+            pltpu.VMEM((count, n1, n2 * rows, cols), BF),
+            pltpu.VMEM((count, slots(n1), n2 * rows, cols), BF),
+            pltpu.VMEM((count, slots(n2), rows, cols), BF),
+        ]
+
+    def semaphores(count, n1, n2):
+        return [
+            pltpu.SemaphoreType.DMA((count, size)) for size in (n1, slots(n1), n2, slots(n2))
+        ]
+
     return pl.pallas_call(
-        functools.partial(weight_kernel, nx, nz, tiles, in_tiles),
-        grid=(tiles + Z_LAG,),
+        functools.partial(weight_kernel, nx, nz, tiles, in_tiles, z_tiles),
+        grid=(tiles + last_lag,),
         in_specs=[
             pl.BlockSpec((tok_rows, width), lambda t: (0, jnp.minimum(t, tiles - 1) // in_tiles)),
             pl.BlockSpec((tok_rows, cols), lambda t: (0, jnp.minimum(t, tiles - 1))),
         ],
         out_specs=[
-            pl.BlockSpec((rows, cols), lambda t: (0, jnp.clip(t - Z_LAG, 0, in_tiles - 1))),
-            pl.BlockSpec((rows, cols), lambda t: (0, jnp.clip(t - Z_LAG - in_tiles, 0, out_tiles - 1))),
+            pl.BlockSpec((rows, cols), lambda t: (0, jnp.clip(t - last_lag, 0, in_tiles - 1))),
+            pl.BlockSpec((rows, cols), lambda t: (0, jnp.clip(t - last_lag - in_tiles, 0, out_tiles - 1))),
         ],
         out_shape=[
             jax.ShapeDtypeStruct((rows, wide), F32),
             jax.ShapeDtypeStruct((rows, width), F32),
         ],
-        scratch_shapes=[
-            pltpu.VMEM((tiles, nx, nz * rows, cols), BF),
-            pltpu.VMEM((tiles, nx - 1, nz * rows, cols), BF),
-            pltpu.VMEM((tiles, nz, rows, cols), BF),
-            pltpu.VMEM((tiles, nz - 1, rows, cols), BF),
-            pltpu.SemaphoreType.DMA((tiles, nx - 1)),
-            pltpu.SemaphoreType.DMA((tiles, nx - 1)),
-            pltpu.SemaphoreType.DMA((tiles, nz - 1)),
-            pltpu.SemaphoreType.DMA((tiles, nz - 1)),
-        ],
+        scratch_shapes=buffers(x_tiles, nx, nz) + buffers(z_tiles, nz, nx)
+        + semaphores(x_tiles, nx, nz) + semaphores(z_tiles, nz, nx),
         compiler_params=pltpu.CompilerParams(
             vmem_limit_bytes=VMEM_LIMIT, collective_id=1, has_side_effects=True
         ),

time: 220 us -> 204 us (0.927)
  Pallas kernels: 207 us -> 191 us
    pallas_call x1, Pallas kernels: 123 us -> 111 us  [weight_grads(): pl.pallas_call(functools.partial(weight_kernel, nx, nz, tiles, in_tiles,...]
    pallas_call x1, Pallas kernels: 53.3 us -> 49.1 us  [body(): pl.pallas_call(functools.partial(backward_kernel, rows, section_count), g...]
where the time goes in v1:
time: 204 us; the launch traced here: 203 us
  Pallas kernels  191 us (94%)
  local copies, waits for them, and re-layouts  8.67 us (4%)
  other arithmetic  3.42 us (2%)
    pallas_call x1, Pallas kernels, weight_grads(): pl.pallas_call(functools.partial(weight_kernel, nx, nz, tiles, in_tiles,...  111 us
    pallas_call x1, Pallas kernels, body(): pl.pallas_call(functools.partial(backward_kernel, rows, section_count), g...  49.1 us
    pallas_call x1, Pallas kernels, body(): pl.pallas_call(functools.partial(forward_kernel, rows, dp_count, section_...  30.2 us
    unnamed x11, local copies, waits for them, and re-layouts  4.35 us

profile of v1, /device:TPU:0, one launch (start us, length us, event | category | flops | bytes accessed | tf_op | source)
XLA Modules:
  0.0 203.3 jit_solution(1419590470118476838)
XLA Ops:
  0.6 0.0 copy-start
  0.7 0.1 pad_add_fusion.1
  0.7 0.8 fusion.2
  1.6 0.8 eq.37
  2.3 0.8 pad_add_fusion
  3.2 0.8 compare_convert_fusion.bm_ref
  3.9 0.9 fusion.1.mask_ref
  4.9 0.0 copy-done
  4.9 3.5 %gather_fusion = bf16[768,1024]{1,0:T(8,128)(2,1)} fusion(bf16[768,1024]{1,0:T(8,128)(2,1)S(1)} %copy-done, s32[1024]{0:T(1024)S(1)} %pad_clamp_fusion), kind=kCustom, calls=%fused_computation | custom fusion | bytes 3148800 | tf_op jit(solution)/shard_map/gather | solution.py:511
  8.4 30.2 %forward.1 = (bf16[8,96,1024]{2,1,0:T(8,128)(2,1)}, bf16[768,2048]{1,0:T(8,128)(2,1)}, bf16[768,1024]{1,0:T(8,128)(2,1)}, bf16[768,1024]{1,0:T(8,128)(2,1)}, bf1...) custom-call(bf16[768,1024]{1,0:T(8,128)(2,1)} %bitcast.26, ...), custom_call_target="tpu_custom_call" | custom-call | flops 6442450944 | bytes 41943040 | tf_op jit(solution)/shard_map/forward/pallas_call | solution.py:535
  38.6 49.1 %backward.1 = (bf16[768,1024]{1,0:T(8,128)(2,1)}, bf16[768,5120]{1,0:T(8,128)(2,1)}) custom-call(bf16[768,1024]{1,0:T(8,128)(2,1)} %bitcast.19, bf16[4096,1024]{1,0:T(8,128)(2,1)} %get-tuple-element.20.win_ref, bf16[1024,1024]{1,0:T(8,128)(2,1)} %get-tuple-element.21.wout_ref, bf16[256,256]{1,0:T(8,128)(2,1)} %compare_convert_fusion.bm_ref, ...), custom_call_target="tpu_custom_call" | custom-call | tf_op jit(solution)/shard_map/backward/pallas_call | solution.py:571
  87.7 0.0 copy-start.2
  87.7 111.2 %weights.1 = (f32[128,4096]{1,0:T(8,128)}, f32[128,1024]{1,0:T(8,128)}) custom-call(bf16[768,2048]{1,0:T(8,128)(2,1)} %get-tuple-element.22.xn_ref.left_ref, bf16[768,5120]{1,0:T(8,128)(2,1)} %get-tuple-element.32.right_ref), custom_call_target="tpu_custom_call" | custom-call | tf_op jit(solution)/shard_map/weights/pallas_call | solution.py:473
  199.0 0.0 copy-done.2
  199.0 0.0 copy-start.1
  199.0 1.1 copy.12
  200.1 1.0 copy-done.1
  201.1 0.0 copy-start.3
  201.2 1.3 copy.13
  202.5 0.1 copy-done.3
  202.5 0.8 copy.14
  (4 shorter events, 0.0 us)
Async XLA Ops:
  0.6 4.2 %copy-start = (bf16[768,1024]{1,0:T(8,128)(2,1)S(1)}, bf16[768,1024]{1,0:T(8,128)(2,1)}, u32[]{:S(2)}) copy-start(bf16[768,1024]{1,0:T(8,128)(2,1)} %param.7) | copy-start | bytes 4718596
  87.7 111.3 %copy-start.2 = (bf16[768,1024]{1,0:T(8,128)(2,1)S(1)}, bf16[768,1024]{1,0:T(8,128)(2,1)}, u32[]{:S(2)}) copy-start(bf16[768,1024]{1,0:T(8,128)(2,1)} %get-tuple-element.31) | copy-start | bytes 4718596
  199.0 2.2 %copy-start.1 = (f32[128,4096]{1,0:T(8,128)S(1)}, f32[128,4096]{1,0:T(8,128)}, u32[]{:S(2)}) copy-start(f32[128,4096]{1,0:T(8,128)} %get-tuple-element.33) | copy-start | bytes 6291460
  201.1 1.4 copy-start.3

commit v2 on v1

--- a/solution.py
+++ b/solution.py
@@ -37,6 +37,12 @@
     return jnp.concatenate([part] * copies, axis=0) * mask
 
 
+def fill_blocks(ref, rows):
+    place = lax.broadcasted_iota(jnp.int32, (rows, ref.shape[1]), 1)
+    for lo in range(0, ref.shape[0], rows):
+        ref[lo : lo + rows, :] = jnp.where((place >= lo) & (place < lo + rows), 1.0, 0.0).astype(BF)
+
+
 def norm_stats(values):
     centered = values - jnp.mean(values, axis=-1, keepdims=True)
     variance = jnp.mean(centered * centered, axis=-1, keepdims=True)
@@ -45,39 +51,67 @@
 
 
 def forward_kernel(
-    rows, dp_count, sections, x_ref, w_ref, mask_ref, bm_ref, picked_ref,
+    rows, dp_count, sections, x_ref, w_ref, seg_ref, list_ref, cot_ref,
     win_part_ref, wout_part_ref,
     packed_ref, xy_ref, gate_ref, mhat_ref, vqk_ref, slope_ref, att_ref, sfac_ref, rx_ref, rm_ref,
-    win_t_ref, wout_t_ref, send_sem, recv_sem, own_sem,
+    win_t_ref, wout_t_ref, bm_ref, before_ref, loaded, picked, send_sem, recv_sem, own_sem,
 ):
     step = pl.program_id(0)
-    sender = lax.axis_index("section") == sections - 1
+    last = sections - 1
+    section = lax.axis_index("section")
     me = lax.axis_index("dp")
-    own = pltpu.make_async_copy(picked_ref.at[me], packed_ref.at[me], own_sem)
-
-    def hop(offset):
-        peer = (me + offset) % dp_count
+    share = packed_ref.shape[1]
+
+    def hop(peer):
         return pltpu.make_async_remote_copy(
-            src_ref=picked_ref.at[peer],
+            src_ref=picked.at[pl.ds(pl.multiple_of(peer * share, 16), share)],
             dst_ref=packed_ref.at[me],
-            send_sem=send_sem.at[offset - 1],
-            recv_sem=recv_sem.at[offset - 1],
-            device_id={"dp": peer},
+            send_sem=send_sem.at[peer],
+            recv_sem=recv_sem.at[me],
+            device_id={"dp": peer, "section": last},
             device_id_type=pl.DeviceIdType.MESH,
         )
 
-    @pl.when((step == 0) & sender)
-    def _():
+    def greet(other):
         barrier = pltpu.get_barrier_semaphore()
-        for offset in range(1, dp_count):
+        for peer in range(dp_count):
             pl.semaphore_signal(
-                barrier, inc=1, device_id={"dp": (me + offset) % dp_count},
+                barrier, inc=1, device_id={"dp": peer, "section": other},
                 device_id_type=pl.DeviceIdType.MESH,
             )
-        pl.semaphore_wait(barrier, dp_count - 1)
-        own.start()
-        for offset in range(1, dp_count):
-            hop(offset).start()
+        pl.semaphore_wait(barrier, dp_count)
+
+    @pl.when(step == 0)
+    def _():
+        fill_blocks(bm_ref, rows)
+        place = lax.broadcasted_iota(jnp.int32, before_ref.shape, 1)
+        below = lax.broadcasted_iota(jnp.int32, before_ref.shape, 0)
+        for lo in range(0, before_ref.shape[1], rows):
+            here = (place >= lo) & (place - lo <= below) & (place < lo + rows)
+            kept = jnp.where(here, 1.0 / rows, 0.0)
+            before_ref[...] = kept if lo == 0 else before_ref[...] + kept
+
+        @pl.when(section == last)
+        def _():
+            greet(0)
+
+        @pl.when(section == 0)
+        def _():
+            load = pltpu.make_async_copy(cot_ref, loaded, own_sem)
+            load.start()
+            greet(last)
+            load.wait()
+            count = picked.shape[0]
+            cut = list_ref.shape[1] // 3 if list_ref.shape[1] % 384 == 0 else list_ref.shape[1]
+            for lo in range(0, count, cut):
+                source = lax.broadcasted_iota(jnp.int32, (count, cut), 0)
+                chosen = jnp.where(source == list_ref[:, lo : lo + cut], 1.0, 0.0).astype(BF)
+                picked[lo : lo + cut, :] = t_mm(chosen, loaded[...]).astype(BF)
+
+    @pl.when((step == 1) & (section == 0))
+    def _():
+        for peer in range(dp_count):
+            hop(peer).start()
 
     width = x_ref.shape[1]
     group = bm_ref.shape[0]
@@ -102,7 +136,12 @@
     scale = 1.0 / head_dim ** 0.5
     for micro in range(x_ref.shape[0] // rows):
         r = slice(micro * rows, (micro + 1) * rows)
-        allowed = jnp.concatenate([mask_ref[r, :]] * (group // mask_ref.shape[1]), axis=1)
+        ids = seg_ref[pl.ds(step * (x_ref.shape[0] // rows) + micro, 1), :].astype(F32)
+        ids = jnp.concatenate([ids] * (128 // rows), axis=1)
+        turned = jnp.broadcast_to(ids, (128, 128)).T[:rows]
+        own_id = jnp.concatenate([turned] * (group // 128), axis=1)
+        key_id = jnp.concatenate([ids] * (group // 128), axis=1)
+        allowed = jnp.where(own_id == key_id, before_ref[...], 0.0)
         mixed = []
         for lo in range(0, width, group):
             c = slice(lo, lo + group)
@@ -122,26 +161,30 @@
         rm_ref[r, :] = jnp.broadcast_to(rm, (rows, rm_ref.shape[1]))
         xy_ref[r, width:] = (mhat * gate_ref[r, :].astype(F32)).astype(BF)
 
-    @pl.when((step == pl.num_programs(0) - 1) & sender)
-    def _():
-        own.wait()
-        for offset in range(1, dp_count):
-            back = pltpu.make_async_remote_copy(
-                src_ref=picked_ref.at[me],
-                dst_ref=packed_ref.at[(me + dp_count - offset) % dp_count],
-                send_sem=send_sem.at[offset - 1],
-                recv_sem=recv_sem.at[offset - 1],
-                device_id={"dp": (me + offset) % dp_count},
-                device_id_type=pl.DeviceIdType.MESH,
-            )
-            back.wait_recv()
-            hop(offset).wait_send()
+    @pl.when(step == pl.num_programs(0) - 1)
+    def _():
+        @pl.when(section == 0)
+        def _():
+            for peer in range(dp_count):
+                hop(peer).wait_send()
+
+        @pl.when(section == last)
+        def _():
+            for peer in range(dp_count):
+                pltpu.make_async_remote_copy(
+                    src_ref=picked.at[pl.ds(0, share)],
+                    dst_ref=packed_ref.at[peer],
+                    send_sem=send_sem.at[peer],
+                    recv_sem=recv_sem.at[peer],
+                    device_id={"dp": peer, "section": 0},
+                    device_id_type=pl.DeviceIdType.MESH,
+                ).wait_recv()
 
 
 def backward_kernel(
-    rows, sections, g0_ref, win_ref, wout_ref, bm_ref, xn_ref, gate_ref, mhat_ref, vqk_ref,
+    rows, sections, g0_ref, win_ref, wout_ref, xn_ref, gate_ref, mhat_ref, vqk_ref,
     slope_ref, att_ref, sfac_ref, rx_ref, rm_ref,
-    dx_ref, dpre_ref, arrived, leaving, send_sem, recv_sem,
+    dx_ref, dpre_ref, bm_ref, arrived, leaving, send_sem, recv_sem,
 ):
     step = pl.program_id(0)
     steps = pl.num_programs(0)
@@ -166,6 +209,7 @@
 
     @pl.when(step == 0)
     def _():
+        fill_blocks(bm_ref, rows)
         barrier = pltpu.get_barrier_semaphore()
 
         @pl.when(section > 0)
@@ -508,23 +552,12 @@
     share = tok_rows // dp_count
     group = rows * (256 // (width // H))
     wide = 4 * width
-    picked = cotangent[pack_lists[0]]
-    positions = jnp.arange(rows)
-    allowed = (segment_ids[:, :, None] == jnp.concatenate([segment_ids] * 2, axis=1)[:, None, :]) & (
-        jnp.concatenate([positions] * 2)[None, None, :] <= positions[None, :, None]
-    )
-    mask = (allowed.astype(F32) / rows).reshape(tok_rows, 2 * rows)
-    blocks = jnp.arange(group) // rows
-    block_mask = (blocks[:, None] == blocks[None, :]).astype(BF)
 
     def row_spec(tile, cols):
         return pl.BlockSpec((tile, cols), lambda i: (i, 0))
 
     def whole_spec(shape):
         return pl.BlockSpec(shape, lambda i: (0, 0), pipeline_mode=pl.Buffered(1))
-
-    def whole_spec3(shape):
-        return pl.BlockSpec(shape, lambda i: (0, 0, 0), pipeline_mode=pl.Buffered(1))
 
     tile = rows * pick(micro_count, F_BATCHES)
     f_steps = tok_rows // tile
@@ -537,8 +570,8 @@
         grid=(tok_rows // tile,),
         in_specs=[
             row_spec(tile, width), whole_spec((width, wide)),
-            row_spec(tile, 2 * rows), whole_spec((group, group)),
-            whole_spec3((dp_count, share, width)),
+            whole_spec((micro_count, rows)), whole_spec((1, tok_rows)),
+            pl.BlockSpec(memory_space=pl.ANY),
             pl.BlockSpec((width, wide // f_steps), lambda i: (0, i)),
             pl.BlockSpec((width // f_steps, width), lambda i: (i, 0)),
         ],
@@ -550,8 +583,12 @@
         + [jax.ShapeDtypeStruct((tok_rows, n), t) for n, t in cols]
         + [jax.ShapeDtypeStruct((wide, width), BF), jax.ShapeDtypeStruct((width, width), BF)],
         scratch_shapes=[
-            pltpu.SemaphoreType.DMA((dp_count - 1,)),
-            pltpu.SemaphoreType.DMA((dp_count - 1,)),
+            pltpu.VMEM((group, group), BF),
+            pltpu.VMEM((rows, group), F32),
+            pltpu.VMEM((tok_rows, width), BF),
+            pltpu.VMEM((tok_rows, width), BF),
+            pltpu.SemaphoreType.DMA((dp_count,)),
+            pltpu.SemaphoreType.DMA((dp_count,)),
             pltpu.SemaphoreType.DMA,
         ],
         compiler_params=pltpu.CompilerParams(
@@ -562,7 +599,7 @@
         ),
         name="forward",
     )(
-        saved_inputs[0], w_in[0], mask, block_mask, picked.reshape(dp_count, share, width),
+        saved_inputs[0], w_in[0], segment_ids, pack_lists, cotangent,
         w_in[0], w_out[0],
     )
 
@@ -573,7 +610,7 @@
         grid=(steps,),
         in_specs=[
             row_spec(tile, width), whole_spec((wide, width)), whole_spec((width, width)),
-            whole_spec((group, group)), row_spec(tile, width), row_spec(tile, width),
+            row_spec(tile, width), row_spec(tile, width),
             row_spec(tile, width), row_spec(tile, 3 * width), row_spec(tile, wide),
             row_spec(tile, width), row_spec(tile, width), row_spec(tile, 128), row_spec(tile, 128),
         ],
@@ -583,6 +620,7 @@
             jax.ShapeDtypeStruct((tok_rows, wide + width), BF),
         ],
         scratch_shapes=[
+            pltpu.VMEM((group, group), BF),
             pltpu.VMEM((steps, tile, width), BF),
             pltpu.VMEM((steps, tile, width), BF),
             pltpu.SemaphoreType.DMA((steps,)),
@@ -592,7 +630,7 @@
             vmem_limit_bytes=VMEM_LIMIT, collective_id=0, has_side_effects=True
         ),
         name="backward",
-    )(packed.reshape(tok_rows, width), win_t, wout_t, block_mask, xy, gate, mhat, vqk, slope, att, sfac, rx, rm)
+    )(packed.reshape(tok_rows, width), win_t, wout_t, xy, gate, mhat, vqk, slope, att, sfac, rx, rm)
 
     grad_w_in, grad_w_out = weight_grads(xy, dgrad, dp_count)
     return (dx[None], grad_w_in[None], grad_w_out[None])

time: 204 us -> 206 us (level)
  Pallas kernels: 191 us -> 200 us
  local copies, waits for them, and re-layouts: 8.67 us -> 4.33 us
  other arithmetic: 3.42 us -> 0 us
    pallas_call x1, Pallas kernels: 30.2 us -> 39.7 us  [body(): pl.pallas_call(functools.partial(forward_kernel, rows, dp_count, section_...]
    pallas_call x1, Pallas kernels: 111 us -> 116 us  [weight_grads(): pl.pallas_call(functools.partial(weight_kernel, nx, nz, tiles, in_tiles,...]
    pallas_call x1, Pallas kernels: 49.1 us -> 44.5 us  [body(): pl.pallas_call(functools.partial(backward_kernel, rows, section_count), g...]
    gather x1 -> x0, local copies, waits for them, and re-layouts: 3.55 us -> none  [body(): picked = cotangent[pack_lists[0]]]
    unnamed x11 -> x9, local copies, waits for them, and re-layouts: 4.35 us -> 4.33 us
where the time goes in v2:
time: 206 us; the launch traced here: 205 us
  Pallas kernels  200 us (97%)
  local copies, waits for them, and re-layouts  4.33 us (2%)
    pallas_call x1, Pallas kernels, weight_grads(): pl.pallas_call(functools.partial(weight_kernel, nx, nz, tiles, in_tiles,...  116 us
    pallas_call x1, Pallas kernels, body(): pl.pallas_call(functools.partial(backward_kernel, rows, section_count), g...  44.5 us
    pallas_call x1, Pallas kernels, body(): pl.pallas_call(functools.partial(forward_kernel, rows, dp_count, section_...  39.7 us
    unnamed x9, local copies, waits for them, and re-layouts  4.33 us

profile of v2, /device:TPU:0, one launch (start us, length us, event | category | flops | bytes accessed | tf_op | source)
XLA Modules:
  0.0 205.5 jit_solution(1675398192003063345)
XLA Ops:
  0.6 39.7 %forward.1 = (bf16[8,96,1024]{2,1,0:T(8,128)(2,1)}, bf16[768,2048]{1,0:T(8,128)(2,1)}, bf16[768,1024]{1,0:T(8,128)(2,1)}, bf16[768,1024]{1,0:T(8,128)(2,1)}, bf1...) custom-call(bf16[768,1024]{1,0:T(8,128)(2,1)} %bitcast.14, ...), custom_call_target="tpu_custom_call" | custom-call | flops 6442450944 | bytes 41943040 | tf_op jit(solution)/shard_map/forward/pallas_call | solution.py:568
  40.3 44.5 %backward.1 = (bf16[768,1024]{1,0:T(8,128)(2,1)}, bf16[768,5120]{1,0:T(8,128)(2,1)}) custom-call(bf16[768,1024]{1,0:T(8,128)(2,1)} %bitcast.8, bf16[4096,1024]{1,0:T(8,128)(2,1)} %get-tuple-element.20.win_ref, bf16[1024,1024]{1,0:T(8,128)(2,1)} %get-tuple-element.21.wout_ref, bf16[768,2048]{1,0:T(8,128)(2,1)} %get-tuple-element.22.xn_ref.left_ref, ...), custom_call_target="tpu_custom_call" | custom-call | tf_op jit(solution)/shard_map/backward/pallas_call | solution.py:608
  84.8 0.0 copy-start.1
  84.8 116.3 %weights.1 = (f32[128,4096]{1,0:T(8,128)}, f32[128,1024]{1,0:T(8,128)}) custom-call(bf16[768,2048]{1,0:T(8,128)(2,1)} %get-tuple-element.22.xn_ref.left_ref, bf16[768,5120]{1,0:T(8,128)(2,1)} %get-tuple-element.32.right_ref), custom_call_target="tpu_custom_call" | custom-call | tf_op jit(solution)/shard_map/weights/pallas_call | solution.py:517
  201.1 0.0 copy-start
  201.1 0.0 copy-done.1
  201.2 1.1 copy.12
  202.3 1.0 copy-done
  203.3 0.0 copy-start.2
  203.3 1.3 copy.13
  204.6 0.1 copy-done.2
  204.7 0.8 copy.14
Async XLA Ops:
  84.8 116.3 %copy-start.1 = (bf16[768,1024]{1,0:T(8,128)(2,1)S(1)}, bf16[768,1024]{1,0:T(8,128)(2,1)}, u32[]{:S(2)}) copy-start(bf16[768,1024]{1,0:T(8,128)(2,1)} %get-tuple-element.31) | copy-start | bytes 4718596
  201.1 2.2 %copy-start = (f32[128,4096]{1,0:T(8,128)S(1)}, f32[128,4096]{1,0:T(8,128)}, u32[]{:S(2)}) copy-start(f32[128,4096]{1,0:T(8,128)} %get-tuple-element.33) | copy-start | bytes 6291460
  203.3 1.4 copy-start.2

commit v3 on v2

--- a/solution.py
+++ b/solution.py
@@ -58,6 +58,7 @@
 ):
     step = pl.program_id(0)
     last = sections - 1
+    picker = sections - 2
     section = lax.axis_index("section")
     me = lax.axis_index("dp")
     share = packed_ref.shape[1]
@@ -93,9 +94,9 @@
 
         @pl.when(section == last)
         def _():
-            greet(0)
-
-        @pl.when(section == 0)
+            greet(picker)
+
+        @pl.when(section == picker)
         def _():
             load = pltpu.make_async_copy(cot_ref, loaded, own_sem)
             load.start()
@@ -107,11 +108,8 @@
                 source = lax.broadcasted_iota(jnp.int32, (count, cut), 0)
                 chosen = jnp.where(source == list_ref[:, lo : lo + cut], 1.0, 0.0).astype(BF)
                 picked[lo : lo + cut, :] = t_mm(chosen, loaded[...]).astype(BF)
-
-    @pl.when((step == 1) & (section == 0))
-    def _():
-        for peer in range(dp_count):
-            hop(peer).start()
+            for offset in range(dp_count):
+                hop((me + offset) % dp_count).start()
 
     width = x_ref.shape[1]
     group = bm_ref.shape[0]
@@ -163,7 +161,7 @@
 
     @pl.when(step == pl.num_programs(0) - 1)
     def _():
-        @pl.when(section == 0)
+        @pl.when(section == picker)
         def _():
             for peer in range(dp_count):
                 hop(peer).wait_send()
@@ -176,7 +174,7 @@
                     dst_ref=packed_ref.at[peer],
                     send_sem=send_sem.at[peer],
                     recv_sem=recv_sem.at[peer],
-                    device_id={"dp": peer, "section": 0},
+                    device_id={"dp": peer, "section": picker},
                     device_id_type=pl.DeviceIdType.MESH,
                 ).wait_recv()
 

time: 206 us -> 199 us (0.966)
  Pallas kernels: 200 us -> 194 us
    pallas_call x1, Pallas kernels: 39.7 us -> 30.9 us  [body(): pl.pallas_call(functools.partial(forward_kernel, rows, dp_count, section_...]
    pallas_call x1, Pallas kernels: 44.5 us -> 51.1 us  [body(): pl.pallas_call(functools.partial(backward_kernel, rows, section_count), g...]
    pallas_call x1, Pallas kernels: 116 us -> 112 us  [weight_grads(): pl.pallas_call(functools.partial(weight_kernel, nx, nz, tiles, in_tiles,...]
where the time goes in v3:
time: 199 us
  Pallas kernels  194 us (97%)
  local copies, waits for them, and re-layouts  4.33 us (2%)
    pallas_call x1, Pallas kernels, weight_grads(): pl.pallas_call(functools.partial(weight_kernel, nx, nz, tiles, in_tiles,...  112 us
    pallas_call x1, Pallas kernels, body(): pl.pallas_call(functools.partial(backward_kernel, rows, section_count), g...  51.1 us
    pallas_call x1, Pallas kernels, body(): pl.pallas_call(functools.partial(forward_kernel, rows, dp_count, section_...  30.9 us
    unnamed x9, local copies, waits for them, and re-layouts  4.33 us

profile of v3, /device:TPU:0, one launch (start us, length us, event | category | flops | bytes accessed | tf_op | source)
XLA Modules:
  0.0 198.6 jit_solution(592390272775950291)
XLA Ops:
  0.6 30.9 %forward.1 = (bf16[8,96,1024]{2,1,0:T(8,128)(2,1)}, bf16[768,2048]{1,0:T(8,128)(2,1)}, bf16[768,1024]{1,0:T(8,128)(2,1)}, bf16[768,1024]{1,0:T(8,128)(2,1)}, bf1...) custom-call(bf16[768,1024]{1,0:T(8,128)(2,1)} %bitcast.14, ...), custom_call_target="tpu_custom_call" | custom-call | flops 6442450944 | bytes 41943040 | tf_op jit(solution)/shard_map/forward/pallas_call | solution.py:566
  31.6 51.1 %backward.1 = (bf16[768,1024]{1,0:T(8,128)(2,1)}, bf16[768,5120]{1,0:T(8,128)(2,1)}) custom-call(bf16[768,1024]{1,0:T(8,128)(2,1)} %bitcast.8, bf16[4096,1024]{1,0:T(8,128)(2,1)} %get-tuple-element.20.win_ref, bf16[1024,1024]{1,0:T(8,128)(2,1)} %get-tuple-element.21.wout_ref, bf16[768,2048]{1,0:T(8,128)(2,1)} %get-tuple-element.22.xn_ref.left_ref, ...), custom_call_target="tpu_custom_call" | custom-call | tf_op jit(solution)/shard_map/backward/pallas_call | solution.py:606
  82.7 0.0 copy-start.1
  82.7 111.6 %weights.1 = (f32[128,4096]{1,0:T(8,128)}, f32[128,1024]{1,0:T(8,128)}) custom-call(bf16[768,2048]{1,0:T(8,128)(2,1)} %get-tuple-element.22.xn_ref.left_ref, bf16[768,5120]{1,0:T(8,128)(2,1)} %get-tuple-element.32.right_ref), custom_call_target="tpu_custom_call" | custom-call | tf_op jit(solution)/shard_map/weights/pallas_call | solution.py:515
  194.3 0.0 copy-start
  194.3 0.0 copy-done.1
  194.3 1.1 copy.12
  195.5 1.0 copy-done
  196.5 0.0 copy-start.2
  196.5 1.3 copy.13
  197.8 0.1 copy-done.2
  197.9 0.8 copy.14
Async XLA Ops:
  82.7 111.6 %copy-start.1 = (bf16[768,1024]{1,0:T(8,128)(2,1)S(1)}, bf16[768,1024]{1,0:T(8,128)(2,1)}, u32[]{:S(2)}) copy-start(bf16[768,1024]{1,0:T(8,128)(2,1)} %get-tuple-element.31) | copy-start | bytes 4718596
  194.3 2.2 %copy-start = (f32[128,4096]{1,0:T(8,128)S(1)}, f32[128,4096]{1,0:T(8,128)}, u32[]{:S(2)}) copy-start(f32[128,4096]{1,0:T(8,128)} %get-tuple-element.33) | copy-start | bytes 6291460
  196.5 1.4 copy-start.2
